TPU v7x, 32 devices: a whole 2x2x4 slice. The times are simulated.
32 devices in a mesh: seq: 8 (over y, x, core), head: 4 (over z).
Axes of the slice: x: 2, y: 2, z: 4, core: 2. Of those that a mesh axis runs over, the one named last changes fastest.
Arguments:
- projected: bfloat16 [4096, 3, 3072], P(('seq', 'head')), may hold values from -70 to 70
- key_lists: int32 [48, 32, 8], P('head', 'seq'), may hold values from 0 to 31, as said below
- list_counts: int32 [48, 32], P('head', 'seq'), may hold values from 1 to 8
Outputs:
- attended: bfloat16 [4096, 3072], P(('seq', 'head'))
Inputs may be any that keep to these rules, and one draw needn't show every extreme that they name: `key_lists`: entries are key block numbers; no list names its own query block, and the entries of one list are distinct. Entry j of the list of query block b in head h lies on seq shard (b // 4 + o + j) mod 8, o depending on h and b. Over the 12 heads of one head group and the query blocks of one seq shard, exactly 48 entries lie on each seq shard, entries past a list's count included, and the entries that lie on one seq shard name at most two distinct key blocks: at most one whose number within its shard is below 2 and at most one whose number is at least that. In every draw some head group, seq shard and owning seq shard have two.
All inputs are finite; a program needn't handle non-finite values.
Results may differ from a plain program's by a relative error of at most 0.005.
Values may be sent and summed in bfloat16 or wider, within the bound.
No kernel may reach another device: no remote copies, remote signals or barrier semaphores. Data moves between devices by JAX's collectives and lax.ppermute only.
A program may use at most 128 MiB of HBM per device.

v0:
```python
import math
import jax
import jax.numpy as jnp
from jax import lax
from jax.sharding import PartitionSpec as P

NEG_FILL = -1e30


def attend_rows(query_part, gathered, live_cols, head_size):
    row_count, seen_blocks, block_len, doubled = gathered.shape
    key_rows = gathered[..., :head_size].reshape(row_count, seen_blocks * block_len, head_size)
    value_rows = gathered[..., head_size:].reshape(row_count, seen_blocks * block_len, head_size)
    attention_scores = jnp.einsum(
        "rqd,rkd->rqk", query_part, key_rows, preferred_element_type=jnp.float32
    ) * (1.0 / math.sqrt(head_size))
    attention_scores = attention_scores.reshape(row_count, block_len, seen_blocks, block_len)
    attention_scores = jnp.where(live_cols[:, None, :, None], attention_scores, NEG_FILL)
    row_top = jnp.max(attention_scores, axis=(2, 3), keepdims=True)
    exp_scores = jnp.exp(attention_scores - row_top)
    attention_weights = (exp_scores / jnp.sum(exp_scores, axis=(2, 3), keepdims=True)).astype(
        jnp.bfloat16
    )
    attention_weights = attention_weights.reshape(row_count, block_len, seen_blocks * block_len)
    return jnp.einsum(
        "rqk,rkd->rqd", attention_weights, value_rows, preferred_element_type=jnp.float32
    )


def on_device(projected, key_lists, list_counts):
    seq_count = lax.axis_size("seq")
    heads_dev, blocks_dev, list_most = key_lists.shape
    regrouped = lax.all_to_all(projected, "head", split_axis=2, concat_axis=0, tiled=True)
    block_len = regrouped.shape[0] // blocks_dev
    group_width = regrouped.shape[2]
    head_size = group_width // heads_dev
    row_count = heads_dev * blocks_dev
    splitted = regrouped.reshape(blocks_dev, block_len, 3, heads_dev, head_size)
    queries = splitted[:, :, 0].transpose(2, 0, 1, 3).reshape(row_count, block_len, head_size)
    kv_pairs = jnp.concatenate([splitted[:, :, 1], splitted[:, :, 2]], axis=-1)
    kv_pairs = kv_pairs.transpose(2, 0, 1, 3).reshape(row_count, block_len, 2 * head_size)
    entries = key_lists.reshape(row_count * list_most)
    owners = entries // blocks_dev
    row_head = jnp.arange(row_count * list_most, dtype=jnp.int32) // (blocks_dev * list_most)
    capacity = row_count * list_most // seq_count
    wanted = row_head * blocks_dev + entries % blocks_dev
    onehot = (owners[:, None] == jnp.arange(seq_count, dtype=jnp.int32)[None, :]).astype(jnp.int32)
    within = jnp.sum(onehot * (jnp.cumsum(onehot, axis=0) - 1), axis=1)
    slot_ids = owners * capacity + within
    request = (
        jnp.zeros((seq_count * capacity,), jnp.int32)
        .at[slot_ids]
        .set(wanted)
        .reshape(seq_count, capacity)
    )
    asked_for = lax.all_to_all(request, "seq", split_axis=0, concat_axis=0, tiled=True)
    served = jnp.take(kv_pairs, asked_for.reshape(-1), axis=0).reshape(
        seq_count, capacity, block_len, 2 * head_size
    )
    fetched = lax.all_to_all(served, "seq", split_axis=0, concat_axis=0, tiled=True)
    fetched = fetched.reshape(seq_count * capacity, block_len, 2 * head_size)
    entry_slots = slot_ids.reshape(row_count, list_most)
    row_counts = list_counts.reshape(row_count)
    group_rows = 4

    def one_group(group_index):
        start = group_index * group_rows
        query_part = lax.dynamic_slice_in_dim(queries, start, group_rows, 0)
        own_pairs = lax.dynamic_slice_in_dim(kv_pairs, start, group_rows, 0)
        slot_part = lax.dynamic_slice_in_dim(entry_slots, start, group_rows, 0)
        count_part = lax.dynamic_slice_in_dim(row_counts, start, group_rows, 0)
        listed = jnp.take(fetched, slot_part.reshape(-1), axis=0).reshape(
            group_rows, list_most, block_len, 2 * head_size
        )
        gathered = jnp.concatenate([own_pairs[:, None], listed], axis=1)
        live_cols = jnp.concatenate(
            [
                jnp.ones((group_rows, 1), bool),
                jnp.arange(list_most, dtype=jnp.int32)[None, :] < count_part[:, None],
            ],
            axis=1,
        )
        return attend_rows(query_part, gathered, live_cols, head_size).astype(jnp.bfloat16)

    attended = lax.map(one_group, jnp.arange(row_count // group_rows, dtype=jnp.int32))
    attended = attended.reshape(row_count, block_len, head_size)
    laid_out = attended.reshape(heads_dev, blocks_dev * block_len, head_size).transpose(1, 0, 2)
    laid_out = laid_out.reshape(blocks_dev * block_len, group_width)
    return lax.all_to_all(laid_out, "head", split_axis=0, concat_axis=1, tiled=True)


def solution(mesh):
    return jax.shard_map(
        on_device,
        mesh=mesh,
        in_specs=(P(("seq", "head"), None, None), P("head", "seq", None), P("head", "seq")),
        out_specs=P(("seq", "head"), None),
        check_vma=False,
    )
```

profile of v0, /device:TPU:2, one launch (start us, length us, event | category | flops | bytes accessed | tf_op | source)
XLA Modules:
  0.0 542.2 jit_solution(7548757384802746488)
XLA Ops:
  6.0 4.3 all-to-all-start.1
  10.3 5.7 %copy.35 = bf16[128,3,3072]{0,1,2:T(4,128)(2,1)} copy(bf16[128,3,3072]{2,0,1:T(8,128)(2,1)} %param.5) | data formatting | bytes 4718592 | tf_op args[0]
  16.0 4.9 all-to-all-start
  22.1 69.7 %all-to-all-done = bf16[128,3,3072]{0,1,2:T(4,128)(2,1)S(1)} async-done(((bf16[128,3,3072]{0,1,2:T(4,128)(2,1)}), bf16[128,3,3072]{0,1,2:T(4,128)(2,1)S(1)}, u32[]{:S(2)}, u32[]{:S(2)}) %all-to-all-start) | async-done | bytes 2359328 | tf_op jit(solution)/shard_map/all_to_all | solution.py:33
  94.5 11.3 %gather_fusion.1 = bf16[384,128,128]{2,1,0:T(8,128)(2,1)} fusion(bf16[48,128,128]{2,1,0:T(8,128)(2,1)S(1)} %bitcast.78, s32[1024]{0:T(1024)S(1)} %pad_clamp_fusion.1), kind=kCustom, calls=%fused_computation.1 | custom fusion | bytes 25167360 | tf_op jit(solution)/shard_map/jit(_take)/gather | solution.py:57
  105.8 10.8 %broadcast_select_fusion.1 = bf16[8,48,128,128]{3,2,1,0:T(8,128)(2,1)} fusion(bf16[8,48,128,128]{3,2,1,0:T(8,128)(2,1)} %bitcast.81, pred[8,48]{1,0:T(8,128)(4,1)S(1)} %compare_and_fusion.1), kind=kLoop, calls=%fused_computation.39 | loop fusion | flops 6291456 | bytes 25166208 | tf_op jit(solution)/shard_map/jit(_take)/select_n | solution.py:57
  116.6 5.7 %all-to-all-start.2 = ((bf16[8,48,128,128]{3,2,1,0:T(8,128)(2,1)}), bf16[8,48,128,128]{3,2,1,0:T(8,128)(2,1)}, u32[]{:S(2)}, u32[]{:S(2)}) async-start(bf16[8,48,128,128]{3,2,1,0:T(8,128)(2,1)} %broadcast_select_fusion.1), calls=%async_computation.2 | async-start | bytes 25165824 | tf_op jit(solution)/shard_map/all_to_all | solution.py:60
  123.6 136.3 %all-to-all-done.2 = bf16[8,48,128,128]{3,2,1,0:T(8,128)(2,1)} async-done(((bf16[8,48,128,128]{3,2,1,0:T(8,128)(2,1)}), bf16[8,48,128,128]{3,2,1,0:T(8,128)(2,1)}, u32[]{:S(2)}, u32[]{:S(2)}) %all-to-all-start.2) | async-done | bytes 12582944 | tf_op jit(solution)/shard_map/all_to_all | solution.py:60
  259.9 256.2 %while.10 = (s32[]{:T(128)}, bf16[12,4,128,64]{2,1,3,0:T(4,128)(2,1)}, s32[12]{0:T(128)S(1)}, s32[48]{0:T(128)S(1)}, bf16[48,128,64]{1,2,0:T(8,128)(2,1)}, /*ind...) while((s32[]{:T(128)}, ...), condition=%wide.region_7.8_spmd, body=%wide.region_4.7_spmd.sunk | while | flops 234721344 | bytes 13664708 | solution.py:85
  261.2 6.3 %gather_fusion = bf16[32,128,128]{2,1,0:T(8,128)(2,1)} fusion(bf16[384,128,128]{2,1,0:T(8,128)(2,1)} %get-tuple-element.162, s32[1024]{0:T(1024)S(1)} %pad_clamp_fusion.3), kind=kCustom, calls=%fused_computation.clone.1 | custom fusion | bytes 2097280 | tf_op jit(solution)/shard_map/while/body/eval_jaxpr/jit(_take)/gather | solution.py:72
  270.6 3.0 fusion.71
  282.6 6.3 %gather_fusion = bf16[32,128,128]{2,1,0:T(8,128)(2,1)} fusion(bf16[384,128,128]{2,1,0:T(8,128)(2,1)} %get-tuple-element.162, s32[1024]{0:T(1024)S(1)} %pad_clamp_fusion.3), kind=kCustom, calls=%fused_computation.clone.1 | custom fusion | bytes 2097280 | tf_op jit(solution)/shard_map/while/body/eval_jaxpr/jit(_take)/gather | solution.py:72
  292.0 3.0 fusion.71
  303.9 6.3 %gather_fusion = bf16[32,128,128]{2,1,0:T(8,128)(2,1)} fusion(bf16[384,128,128]{2,1,0:T(8,128)(2,1)} %get-tuple-element.162, s32[1024]{0:T(1024)S(1)} %pad_clamp_fusion.3), kind=kCustom, calls=%fused_computation.clone.1 | custom fusion | bytes 2097280 | tf_op jit(solution)/shard_map/while/body/eval_jaxpr/jit(_take)/gather | solution.py:72
  313.3 3.0 fusion.71
  325.3 6.3 %gather_fusion = bf16[32,128,128]{2,1,0:T(8,128)(2,1)} fusion(bf16[384,128,128]{2,1,0:T(8,128)(2,1)} %get-tuple-element.162, s32[1024]{0:T(1024)S(1)} %pad_clamp_fusion.3), kind=kCustom, calls=%fused_computation.clone.1 | custom fusion | bytes 2097280 | tf_op jit(solution)/shard_map/while/body/eval_jaxpr/jit(_take)/gather | solution.py:72
  334.7 3.0 fusion.71
  346.6 6.3 %gather_fusion = bf16[32,128,128]{2,1,0:T(8,128)(2,1)} fusion(bf16[384,128,128]{2,1,0:T(8,128)(2,1)} %get-tuple-element.162, s32[1024]{0:T(1024)S(1)} %pad_clamp_fusion.3), kind=kCustom, calls=%fused_computation.clone.1 | custom fusion | bytes 2097280 | tf_op jit(solution)/shard_map/while/body/eval_jaxpr/jit(_take)/gather | solution.py:72
  356.0 3.0 fusion.71
  368.0 6.3 %gather_fusion = bf16[32,128,128]{2,1,0:T(8,128)(2,1)} fusion(bf16[384,128,128]{2,1,0:T(8,128)(2,1)} %get-tuple-element.162, s32[1024]{0:T(1024)S(1)} %pad_clamp_fusion.3), kind=kCustom, calls=%fused_computation.clone.1 | custom fusion | bytes 2097280 | tf_op jit(solution)/shard_map/while/body/eval_jaxpr/jit(_take)/gather | solution.py:72
  377.4 3.0 fusion.71
  389.3 6.3 %gather_fusion = bf16[32,128,128]{2,1,0:T(8,128)(2,1)} fusion(bf16[384,128,128]{2,1,0:T(8,128)(2,1)} %get-tuple-element.162, s32[1024]{0:T(1024)S(1)} %pad_clamp_fusion.3), kind=kCustom, calls=%fused_computation.clone.1 | custom fusion | bytes 2097280 | tf_op jit(solution)/shard_map/while/body/eval_jaxpr/jit(_take)/gather | solution.py:72
  398.7 3.0 fusion.71
  410.7 6.3 %gather_fusion = bf16[32,128,128]{2,1,0:T(8,128)(2,1)} fusion(bf16[384,128,128]{2,1,0:T(8,128)(2,1)} %get-tuple-element.162, s32[1024]{0:T(1024)S(1)} %pad_clamp_fusion.3), kind=kCustom, calls=%fused_computation.clone.1 | custom fusion | bytes 2097280 | tf_op jit(solution)/shard_map/while/body/eval_jaxpr/jit(_take)/gather | solution.py:72
  432.0 6.3 %gather_fusion = bf16[32,128,128]{2,1,0:T(8,128)(2,1)} fusion(bf16[384,128,128]{2,1,0:T(8,128)(2,1)} %get-tuple-element.162, s32[1024]{0:T(1024)S(1)} %pad_clamp_fusion.3), kind=kCustom, calls=%fused_computation.clone.1 | custom fusion | bytes 2097280 | tf_op jit(solution)/shard_map/while/body/eval_jaxpr/jit(_take)/gather | solution.py:72
  441.4 3.0 fusion.71
  453.4 6.3 %gather_fusion = bf16[32,128,128]{2,1,0:T(8,128)(2,1)} fusion(bf16[384,128,128]{2,1,0:T(8,128)(2,1)} %get-tuple-element.162, s32[1024]{0:T(1024)S(1)} %pad_clamp_fusion.3), kind=kCustom, calls=%fused_computation.clone.1 | custom fusion | bytes 2097280 | tf_op jit(solution)/shard_map/while/body/eval_jaxpr/jit(_take)/gather | solution.py:72
  474.7 6.3 %gather_fusion = bf16[32,128,128]{2,1,0:T(8,128)(2,1)} fusion(bf16[384,128,128]{2,1,0:T(8,128)(2,1)} %get-tuple-element.162, s32[1024]{0:T(1024)S(1)} %pad_clamp_fusion.3), kind=kCustom, calls=%fused_computation.clone.1 | custom fusion | bytes 2097280 | tf_op jit(solution)/shard_map/while/body/eval_jaxpr/jit(_take)/gather | solution.py:72
  484.1 3.0 fusion.71
  496.1 6.3 %gather_fusion = bf16[32,128,128]{2,1,0:T(8,128)(2,1)} fusion(bf16[384,128,128]{2,1,0:T(8,128)(2,1)} %get-tuple-element.162, s32[1024]{0:T(1024)S(1)} %pad_clamp_fusion.3), kind=kCustom, calls=%fused_computation.clone.1 | custom fusion | bytes 2097280 | tf_op jit(solution)/shard_map/while/body/eval_jaxpr/jit(_take)/gather | solution.py:72
  505.5 3.0 fusion.71
  518.0 23.0 %all_to_all.48 = bf16[4,128,768]{1,2,0:T(8,128)(2,1)S(1)} all-to-all(bf16[4,128,768]{1,2,0:T(8,128)(2,1)S(1)} %copy.46), channel_id=1, replica_groups=mesh['seq'=8,'head'=4] {'head'}, dimensions={0} | all-to-all | bytes 1572864 | tf_op jit(solution)/shard_map/all_to_all | solution.py:89
  (272 shorter events, 156.9 us)
Async XLA Ops:
  6.0 9.9 %all-to-all-start.1 = ((s32[8,1,48]{2,1,0:T(1,128)}), s32[8,1,48]{2,1,0:T(1,128)S(1)}, u32[]{:S(2)}, u32[]{:S(2)}) async-start(s32[8,1,48]{2,1,0:T(1,128)} %all_to_all.37), calls=%async_computation.1 | async-start | bytes 8192 | tf_op jit(solution)/shard_map/all_to_all | solution.py:56
  16.0 75.9 %all-to-all-start = ((bf16[128,3,3072]{0,1,2:T(4,128)(2,1)}), bf16[128,3,3072]{0,1,2:T(4,128)(2,1)S(1)}, u32[]{:S(2)}, u32[]{:S(2)}) async-start(bf16[128,3,3072]{0,1,2:T(4,128)(2,1)} %copy.35), calls=%async_computation | async-start | bytes 6291456 | tf_op jit(solution)/shard_map/all_to_all | solution.py:33
  116.6 5.8 %copy-start.1 = (s32[12,4]{0,1:T(4,128)S(1)}, s32[12,4]{0,1:T(4,128)}, u32[]{:S(2)}) copy-start(s32[12,4]{0,1:T(4,128)} %param.7) | copy-start | bytes 580
  116.6 6.0 %copy-start = (bf16[12,4,128,64]{2,3,0,1:T(8,128)(2,1)S(1)}, bf16[12,4,128,64]{2,3,0,1:T(8,128)(2,1)}, u32[]{:S(2)}) copy-start(bf16[12,4,128,64]{2,3,0,1:T(8,128)(2,1)} %get-tuple-element.69) | copy-start | bytes 2359300
  116.6 143.3 %all-to-all-start.2 = ((bf16[8,48,128,128]{3,2,1,0:T(8,128)(2,1)}), bf16[8,48,128,128]{3,2,1,0:T(8,128)(2,1)}, u32[]{:S(2)}, u32[]{:S(2)}) async-start(bf16[8,48,128,128]{3,2,1,0:T(8,128)(2,1)} %broadcast_select_fusion.1), calls=%async_computation.2 | async-start | bytes 25165824 | tf_op jit(solution)/shard_map/all_to_all | solution.py:60
where the time goes:
time: 545 us; the launch traced here: 542 us
  waiting for transfers between devices  206 us (38%)
  local copies, waits for them, and re-layouts  178 us (33%)
  other arithmetic  64.3 us (12%)
  matrix products  47.5 us (9%)
  blocking collectives  23 us (4%)
  starting transfers between devices  14.8 us (3%)
  loops' own time  8.01 us (1%)
    all_to_all x1, waiting for transfers between devices, on_device(): lax.all_to_all(served, 'seq', split_axis=0, concat_axis=0, tiled=True)  136 us
    gather x24, local copies, waits for them, and re-layouts, one_group(): jnp.take(fetched, slot_part.reshape(-1), axis=0)  95.7 us
    all_to_all x1, waiting for transfers between devices, on_device(): lax.all_to_all(projected, 'head', split_axis=2, concat_axis=0, tiled=True)  69.7 us
    concatenate x12, other arithmetic, one_group(): gathered = jnp.concatenate([own_pairs[:, None], listed], axis=1)  35.8 us
    dot_general x12, matrix products, attend_rows(): jnp.einsum('rqk,rkd->rqd', attention_weights, value_rows, preferred_eleme...  26.2 us
    all_to_all x1, blocking collectives, on_device(): lax.all_to_all(laid_out, 'head', split_axis=0, concat_axis=1, tiled=True)  23 us
    sub x12, matrix products, attend_rows(): exp_scores = jnp.exp(attention_scores - row_top)  21.2 us
    reshape x12, local copies, waits for them, and re-layouts, attend_rows(): gathered[..., :head_size]  17.7 us
  transfers between devices with their start and end apart: 3, of which 2 were waited for; matrix products, arithmetic and copies ran while one was open for 2% of the time, Pallas kernels for 0%

commit v1 on v0

--- a/solution.py
+++ b/solution.py
@@ -5,6 +5,29 @@
 from jax.sharding import PartitionSpec as P
 
 NEG_FILL = -1e30
+
+
+def in_blocks(array, dim, size):
+    shape = array.shape
+    blocks = array.reshape(*shape[:dim], size, shape[dim] // size, *shape[dim + 1 :])
+    return jnp.moveaxis(blocks, dim, 0)
+
+
+def laid_out_2(blocks, dim):
+    blocks = jnp.moveaxis(blocks, 0, dim)
+    lengths = blocks.shape
+    return blocks.reshape(*lengths[:dim], lengths[dim] * lengths[dim + 1], *lengths[dim + 2 :])
+
+
+def exchange_in_pairs(shard, axis, split_dim, concat_dim):
+    size, index = (lax.axis_size(axis), lax.axis_index(axis))
+    blocks = in_blocks(shard, split_dim, size)
+    outs = [blocks[index]]
+    for step in range(1, size):
+        sent = blocks[index ^ step]
+        outs.append(lax.ppermute(sent, axis, [(i, i ^ step) for i in range(size)]))
+    blocks = jnp.stack(outs)[index ^ jnp.arange(size)]
+    return laid_out_2(blocks, concat_dim)
 
 
 def attend_rows(query_part, gathered, live_cols, head_size):
@@ -57,7 +80,7 @@
     served = jnp.take(kv_pairs, asked_for.reshape(-1), axis=0).reshape(
         seq_count, capacity, block_len, 2 * head_size
     )
-    fetched = lax.all_to_all(served, "seq", split_axis=0, concat_axis=0, tiled=True)
+    fetched = exchange_in_pairs(served, "seq", 0, 0)
     fetched = fetched.reshape(seq_count * capacity, block_len, 2 * head_size)
     entry_slots = slot_ids.reshape(row_count, list_most)
     row_counts = list_counts.reshape(row_count)

time: 545 us -> 563 us (1.033)
  local copies, waits for them, and re-layouts: 178 us -> 214 us
  waiting for transfers between devices: 206 us -> 192 us
    all_to_all x1 -> x0, waiting for transfers between devices: 136 us -> none  [on_device(): lax.all_to_all(served, 'seq', split_axis=0, concat_axis=0, tiled=True)]
    ppermute x0 -> x7, waiting for transfers between devices: none -> 122 us  [exchange_in_pairs(): outs.append(lax.ppermute(sent, axis, [(i, i ^ step) for i in range(size)]))]
    unnamed x7 -> x13, local copies, waits for them, and re-layouts: 6.61 us -> 23.1 us
    gather x0 -> x1, local copies, waits for them, and re-layouts: none -> 11 us  [exchange_in_pairs(): blocks = jnp.stack(outs)[index ^ jnp.arange(size)]]
    all_to_all x1 -> x0, starting transfers between devices: 5.72 us -> none  [on_device(): lax.all_to_all(served, 'seq', split_axis=0, concat_axis=0, tiled=True)]
  transfers between devices with their start and end apart: 3 -> 9, of which waited for: 2 -> 5; matrix products, arithmetic and copies ran while one was open for 2% -> 4% of each run, Pallas kernels for 0% -> 0%
where the time goes in v1:
time: 563 us; the launch traced here: 559 us
  local copies, waits for them, and re-layouts  214 us (38%)
  waiting for transfers between devices  192 us (34%)
  other arithmetic  60 us (11%)
  matrix products  47.5 us (8%)
  blocking collectives  23.4 us (4%)
  starting transfers between devices  14.4 us (3%)
  loops' own time  8.01 us (1%)
    ppermute x7, waiting for transfers between devices, exchange_in_pairs(): outs.append(lax.ppermute(sent, axis, [(i, i ^ step) for i in range(size)]))  122 us
    gather x24, local copies, waits for them, and re-layouts, one_group(): jnp.take(fetched, slot_part.reshape(-1), axis=0)  95.7 us
    all_to_all x1, waiting for transfers between devices, on_device(): lax.all_to_all(projected, 'head', split_axis=2, concat_axis=0, tiled=True)  69.9 us
    concatenate x12, other arithmetic, one_group(): gathered = jnp.concatenate([own_pairs[:, None], listed], axis=1)  35.8 us
    dot_general x12, matrix products, attend_rows(): jnp.einsum('rqk,rkd->rqd', attention_weights, value_rows, preferred_eleme...  26.2 us
    all_to_all x1, blocking collectives, on_device(): lax.all_to_all(laid_out, 'head', split_axis=0, concat_axis=1, tiled=True)  23.4 us
    unnamed x13, local copies, waits for them, and re-layouts  23.1 us
    sub x12, matrix products, attend_rows(): exp_scores = jnp.exp(attention_scores - row_top)  21.2 us
  transfers between devices with their start and end apart: 9, of which 5 were waited for; matrix products, arithmetic and copies ran while one was open for 4% of the time, Pallas kernels for 0%

profile of v1, /device:TPU:2, one launch (start us, length us, event | category | flops | bytes accessed | tf_op | source)
XLA Modules:
  0.0 559.0 jit_solution(9776444709007312853)
XLA Ops:
  6.0 4.3 all-to-all-start.1
  10.3 5.7 %copy.34 = bf16[128,3,3072]{0,1,2:T(4,128)(2,1)} copy(bf16[128,3,3072]{2,0,1:T(8,128)(2,1)} %param.5) | data formatting | bytes 4718592 | tf_op args[0]
  15.9 4.9 all-to-all-start
  22.1 69.9 %all-to-all-done = bf16[128,3,3072]{0,1,2:T(4,128)(2,1)} async-done(((bf16[128,3,3072]{0,1,2:T(4,128)(2,1)}), bf16[128,3,3072]{0,1,2:T(4,128)(2,1)}, u32[]{:S(2)}, u32[]{:S(2)}) %all-to-all-start) | async-done | bytes 2359328 | tf_op jit(solution)/shard_map/all_to_all | solution.py:56
  96.6 11.3 %gather_fusion.1 = bf16[384,128,128]{2,1,0:T(8,128)(2,1)} fusion(bf16[48,128,128]{2,1,0:T(8,128)(2,1)S(1)} %bitcast.109, s32[1024]{0:T(1024)S(1)} %pad_clamp_fusion.2), kind=kCustom, calls=%fused_computation.1 | custom fusion | bytes 25167360 | tf_op jit(solution)/shard_map/jit(_take)/gather | solution.py:80
  107.9 6.5 %broadcast_select_fusion.1 = bf16[8,1,48,128,128]{4,3,2,0,1:T(8,128)(2,1)S(1)} fusion(bf16[8,1,48,128,128]{4,3,2,0,1:T(8,128)(2,1)} %bitcast.112, pred[8,48]{1,0:T(8,128)(4,1)S(1)} %compare_and_fusion.1), kind=kLoop, calls=%fused_computation.40 | loop fusion | flops 6291456 | bytes 25166208 | tf_op jit(solution)/shard_map/jit(_take)/select_n | solution.py:80
  114.4 4.7 dynamic-slice_bitcast_fusion.1
  125.5 31.2 %collective-permute-done.1 = bf16[1,48,128,128]{3,2,1,0:T(8,128)(2,1)} collective-permute-done((bf16[1,48,128,128]{3,2,1,0:T(8,128)(2,1)}, bf16[1,48,128,128]{3,2,1,0:T(8,128)(2,1)}, u32[]{:S(2)}, u32[]{:S(2)}) %collective-permute-start.1) | collective-permute-done | bytes 1572896 | tf_op jit(solution)/shard_map/ppermute | solution.py:28
  162.4 27.1 %collective-permute-done.2 = bf16[1,48,128,128]{3,2,1,0:T(8,128)(2,1)} collective-permute-done((bf16[1,48,128,128]{3,2,1,0:T(8,128)(2,1)}, bf16[1,48,128,128]{3,2,1,0:T(8,128)(2,1)}, u32[]{:S(2)}, u32[]{:S(2)}) %collective-permute-start.2) | collective-permute-done | bytes 1572896 | tf_op jit(solution)/shard_map/ppermute | solution.py:28
  195.0 63.5 %collective-permute-done.4 = bf16[1,48,128,128]{3,2,1,0:T(8,128)(2,1)} collective-permute-done((bf16[1,48,128,128]{3,2,1,0:T(8,128)(2,1)}, bf16[1,48,128,128]{3,2,1,0:T(8,128)(2,1)}, u32[]{:S(2)}, u32[]{:S(2)}) %collective-permute-start.4) | collective-permute-done | bytes 1572896 | tf_op jit(solution)/shard_map/ppermute | solution.py:28
  265.3 11.0 %gather_fusion.2 = bf16[8,48,128,128]{3,2,1,0:T(8,128)(2,1)} fusion(bf16[8,48,128,128]{3,2,1,0:T(8,128)(2,1)} %bitcast.114, s32[1024]{0:T(1024)S(1)} %pad_clamp_fusion.1), kind=kCustom, calls=%fused_computation.2 | custom fusion | bytes 25165856 | tf_op jit(solution)/shard_map/gather | solution.py:29
  276.3 256.2 %while.10 = (s32[]{:T(128)}, bf16[12,4,128,64]{2,1,3,0:T(4,128)(2,1)}, s32[12]{0:T(128)S(1)}, s32[48]{0:T(128)S(1)}, bf16[48,128,64]{1,2,0:T(8,128)(2,1)}, /*ind...) while((s32[]{:T(128)}, ...), condition=%wide.region_7.8_spmd, body=%wide.region_4.7_spmd.sunk | while | flops 234721344 | bytes 13664708 | solution.py:108
  277.7 6.3 %gather_fusion = bf16[32,128,128]{2,1,0:T(8,128)(2,1)} fusion(bf16[384,128,128]{2,1,0:T(8,128)(2,1)} %get-tuple-element.170, s32[1024]{0:T(1024)S(1)} %pad_clamp_fusion.4), kind=kCustom, calls=%fused_computation.clone.1 | custom fusion | bytes 2097280 | tf_op jit(solution)/shard_map/while/body/eval_jaxpr/jit(_take)/gather | solution.py:95
  287.1 3.0 fusion.72
  299.0 6.3 %gather_fusion = bf16[32,128,128]{2,1,0:T(8,128)(2,1)} fusion(bf16[384,128,128]{2,1,0:T(8,128)(2,1)} %get-tuple-element.170, s32[1024]{0:T(1024)S(1)} %pad_clamp_fusion.4), kind=kCustom, calls=%fused_computation.clone.1 | custom fusion | bytes 2097280 | tf_op jit(solution)/shard_map/while/body/eval_jaxpr/jit(_take)/gather | solution.py:95
  320.4 6.3 %gather_fusion = bf16[32,128,128]{2,1,0:T(8,128)(2,1)} fusion(bf16[384,128,128]{2,1,0:T(8,128)(2,1)} %get-tuple-element.170, s32[1024]{0:T(1024)S(1)} %pad_clamp_fusion.4), kind=kCustom, calls=%fused_computation.clone.1 | custom fusion | bytes 2097280 | tf_op jit(solution)/shard_map/while/body/eval_jaxpr/jit(_take)/gather | solution.py:95
  329.7 3.0 fusion.72
  341.7 6.3 %gather_fusion = bf16[32,128,128]{2,1,0:T(8,128)(2,1)} fusion(bf16[384,128,128]{2,1,0:T(8,128)(2,1)} %get-tuple-element.170, s32[1024]{0:T(1024)S(1)} %pad_clamp_fusion.4), kind=kCustom, calls=%fused_computation.clone.1 | custom fusion | bytes 2097280 | tf_op jit(solution)/shard_map/while/body/eval_jaxpr/jit(_take)/gather | solution.py:95
  351.1 3.0 fusion.72
  363.1 6.3 %gather_fusion = bf16[32,128,128]{2,1,0:T(8,128)(2,1)} fusion(bf16[384,128,128]{2,1,0:T(8,128)(2,1)} %get-tuple-element.170, s32[1024]{0:T(1024)S(1)} %pad_clamp_fusion.4), kind=kCustom, calls=%fused_computation.clone.1 | custom fusion | bytes 2097280 | tf_op jit(solution)/shard_map/while/body/eval_jaxpr/jit(_take)/gather | solution.py:95
  384.4 6.3 %gather_fusion = bf16[32,128,128]{2,1,0:T(8,128)(2,1)} fusion(bf16[384,128,128]{2,1,0:T(8,128)(2,1)} %get-tuple-element.170, s32[1024]{0:T(1024)S(1)} %pad_clamp_fusion.4), kind=kCustom, calls=%fused_computation.clone.1 | custom fusion | bytes 2097280 | tf_op jit(solution)/shard_map/while/body/eval_jaxpr/jit(_take)/gather | solution.py:95
  393.8 3.0 fusion.72
  405.8 6.3 %gather_fusion = bf16[32,128,128]{2,1,0:T(8,128)(2,1)} fusion(bf16[384,128,128]{2,1,0:T(8,128)(2,1)} %get-tuple-element.170, s32[1024]{0:T(1024)S(1)} %pad_clamp_fusion.4), kind=kCustom, calls=%fused_computation.clone.1 | custom fusion | bytes 2097280 | tf_op jit(solution)/shard_map/while/body/eval_jaxpr/jit(_take)/gather | solution.py:95
  427.1 6.3 %gather_fusion = bf16[32,128,128]{2,1,0:T(8,128)(2,1)} fusion(bf16[384,128,128]{2,1,0:T(8,128)(2,1)} %get-tuple-element.170, s32[1024]{0:T(1024)S(1)} %pad_clamp_fusion.4), kind=kCustom, calls=%fused_computation.clone.1 | custom fusion | bytes 2097280 | tf_op jit(solution)/shard_map/while/body/eval_jaxpr/jit(_take)/gather | solution.py:95
  436.5 3.0 fusion.72
  448.4 6.3 %gather_fusion = bf16[32,128,128]{2,1,0:T(8,128)(2,1)} fusion(bf16[384,128,128]{2,1,0:T(8,128)(2,1)} %get-tuple-element.170, s32[1024]{0:T(1024)S(1)} %pad_clamp_fusion.4), kind=kCustom, calls=%fused_computation.clone.1 | custom fusion | bytes 2097280 | tf_op jit(solution)/shard_map/while/body/eval_jaxpr/jit(_take)/gather | solution.py:95
  457.8 3.0 fusion.72
  469.8 6.3 %gather_fusion = bf16[32,128,128]{2,1,0:T(8,128)(2,1)} fusion(bf16[384,128,128]{2,1,0:T(8,128)(2,1)} %get-tuple-element.170, s32[1024]{0:T(1024)S(1)} %pad_clamp_fusion.4), kind=kCustom, calls=%fused_computation.clone.1 | custom fusion | bytes 2097280 | tf_op jit(solution)/shard_map/while/body/eval_jaxpr/jit(_take)/gather | solution.py:95
  479.2 3.0 fusion.72
  491.1 6.3 %gather_fusion = bf16[32,128,128]{2,1,0:T(8,128)(2,1)} fusion(bf16[384,128,128]{2,1,0:T(8,128)(2,1)} %get-tuple-element.170, s32[1024]{0:T(1024)S(1)} %pad_clamp_fusion.4), kind=kCustom, calls=%fused_computation.clone.1 | custom fusion | bytes 2097280 | tf_op jit(solution)/shard_map/while/body/eval_jaxpr/jit(_take)/gather | solution.py:95
  512.5 6.3 %gather_fusion = bf16[32,128,128]{2,1,0:T(8,128)(2,1)} fusion(bf16[384,128,128]{2,1,0:T(8,128)(2,1)} %get-tuple-element.170, s32[1024]{0:T(1024)S(1)} %pad_clamp_fusion.4), kind=kCustom, calls=%fused_computation.clone.1 | custom fusion | bytes 2097280 | tf_op jit(solution)/shard_map/while/body/eval_jaxpr/jit(_take)/gather | solution.py:95
  534.4 23.4 %all_to_all.43 = bf16[4,128,768]{1,2,0:T(8,128)(2,1)S(1)} all-to-all(bf16[4,128,768]{1,2,0:T(8,128)(2,1)S(1)} %copy.45), channel_id=1, replica_groups=mesh['seq'=8,'head'=4] {'head'}, dimensions={0} | all-to-all | bytes 1572864 | tf_op jit(solution)/shard_map/all_to_all | solution.py:112
  (295 shorter events, 190.9 us)
Async XLA Ops:
  6.0 9.9 %all-to-all-start.1 = ((s32[8,1,48]{2,1,0:T(1,128)}), s32[8,1,48]{2,1,0:T(1,128)S(1)}, u32[]{:S(2)}, u32[]{:S(2)}) async-start(s32[8,1,48]{2,1,0:T(1,128)} %all_to_all.34), calls=%async_computation.1 | async-start | bytes 8192 | tf_op jit(solution)/shard_map/all_to_all | solution.py:79
  15.9 76.1 %all-to-all-start = ((bf16[128,3,3072]{0,1,2:T(4,128)(2,1)}), bf16[128,3,3072]{0,1,2:T(4,128)(2,1)}, u32[]{:S(2)}, u32[]{:S(2)}) async-start(bf16[128,3,3072]{0,1,2:T(4,128)(2,1)} %copy.34), calls=%async_computation | async-start | bytes 6291456 | tf_op jit(solution)/shard_map/all_to_all | solution.py:56
  114.4 10.0 %copy-start.1 = (s32[12,4]{0,1:T(4,128)S(1)}, s32[12,4]{0,1:T(4,128)}, u32[]{:S(2)}) copy-start(s32[12,4]{0,1:T(4,128)} %param.7) | copy-start | bytes 580
  114.4 10.1 %copy-start = (bf16[12,4,128,64]{2,3,0,1:T(8,128)(2,1)S(1)}, bf16[12,4,128,64]{2,3,0,1:T(8,128)(2,1)}, u32[]{:S(2)}) copy-start(bf16[12,4,128,64]{2,3,0,1:T(8,128)(2,1)} %get-tuple-element.77) | copy-start | bytes 2359300
  119.1 3.8 collective-permute-start
  119.1 37.6 %collective-permute-start.1 = (bf16[1,48,128,128]{3,2,1,0:T(8,128)(2,1)}, bf16[1,48,128,128]{3,2,1,0:T(8,128)(2,1)}, u32[]{:S(2)}, u32[]{:S(2)}) collective-permute-start(bf16[1,48,128,128]{3,2,1,0:T(8,128)(2,1)} %get-tuple-element.73), channel_id=1, source_target_pairs={{0,8},{4,12},{8,0},{12,4},{16,24},{20,28},{24,16},{28,20},{1,9},{5... | collective-permute-start | bytes 4718600 | tf_op jit(solution)/shard_map/ppermute | solution.py:28
  119.6 70.0 %collective-permute-start.2 = (bf16[1,48,128,128]{3,2,1,0:T(8,128)(2,1)}, bf16[1,48,128,128]{3,2,1,0:T(8,128)(2,1)}, u32[]{:S(2)}, u32[]{:S(2)}) collective-permute-start(bf16[1,48,128,128]{3,2,1,0:T(8,128)(2,1)} %get-tuple-element.72), channel_id=1, source_target_pairs={{0,12},{4,8},{8,4},{12,0},{16,28},{20,24},{24,20},{28,16},{1,13},{... | collective-permute-start | bytes 4718600 | tf_op jit(solution)/shard_map/ppermute | solution.py:28
  121.0 71.3 %collective-permute-start.3 = (bf16[1,48,128,128]{3,2,1,0:T(8,128)(2,1)}, bf16[1,48,128,128]{3,2,1,0:T(8,128)(2,1)}, u32[]{:S(2)}, u32[]{:S(2)}) collective-permute-start(bf16[1,48,128,128]{3,2,1,0:T(8,128)(2,1)} %get-tuple-element.71), channel_id=1, source_target_pairs={{0,16},{4,20},{8,24},{12,28},{16,0},{20,4},{24,8},{28,12},{1,17},{... | collective-permute-start | bytes 4718600 | tf_op jit(solution)/shard_map/ppermute | solution.py:28
  122.5 136.0 %collective-permute-start.4 = (bf16[1,48,128,128]{3,2,1,0:T(8,128)(2,1)}, bf16[1,48,128,128]{3,2,1,0:T(8,128)(2,1)}, u32[]{:S(2)}, u32[]{:S(2)}) collective-permute-start(bf16[1,48,128,128]{3,2,1,0:T(8,128)(2,1)} %get-tuple-element.70), channel_id=1, source_target_pairs={{0,20},{4,16},{8,28},{12,24},{16,4},{20,0},{24,12},{28,8},{1,21},{... | collective-permute-start | bytes 4718600 | tf_op jit(solution)/shard_map/ppermute | solution.py:28
  122.9 138.4 %collective-permute-start.5 = (bf16[1,48,128,128]{3,2,1,0:T(8,128)(2,1)}, bf16[1,48,128,128]{3,2,1,0:T(8,128)(2,1)}, u32[]{:S(2)}, u32[]{:S(2)}) collective-permute-start(bf16[1,48,128,128]{3,2,1,0:T(8,128)(2,1)} %get-tuple-element.69), channel_id=1, source_target_pairs={{0,24},{4,28},{8,16},{12,20},{16,8},{20,12},{24,0},{28,4},{1,25},{... | collective-permute-start | bytes 4718600 | tf_op jit(solution)/shard_map/ppermute | solution.py:28
  156.7 107.3 %collective-permute-start.6 = (bf16[1,48,128,128]{3,2,1,0:T(8,128)(2,1)}, bf16[1,48,128,128]{3,2,1,0:T(8,128)(2,1)S(1)}, u32[]{:S(2)}, u32[]{:S(2)}) collective-permute-start(bf16[1,48,128,128]{3,2,1,0:T(8,128)(2,1)} %get-tuple-element.68), channel_id=1, source_target_pairs={{0,28},{4,24},{8,20},{12,16},{16,12},{20,8},{24,4},{28,0},{1,29},{... | collective-permute-start | bytes 4718600 | tf_op jit(solution)/shard_map/ppermute | solution.py:28
